TPU v7x, 512 devices: a whole 4x8x8 slice. The times are simulated.
512 devices in a mesh: req: 64 (over z, x, core), mdl: 8 (over y).
Axes of the slice: x: 4, y: 8, z: 8, core: 2. Of those that a mesh axis runs over, the one named last changes fastest.
Arguments:
- hidden_in: bfloat16 [8192, 2048], P('req'), may hold values from -6 to 6
- z_weight: bfloat16 [2048, 4096], P('req', 'mdl'), may hold values from -0.125 to 0.125
- x_weight: bfloat16 [2048, 4096], P('req', 'mdl'), may hold values from -0.125 to 0.125
- state_proj: bfloat16 [2048, 256], P('req'), may hold values from -0.125 to 0.125
- step_weight: bfloat16 [2048, 64], P('req', 'mdl'), may hold values from -0.125 to 0.125
- step_bias: float32 [64], P('mdl'), may hold values from -4 to -1
- decay_log: float32 [64], P('mdl'), may hold values from -2 to 1
- skip_gain: float32 [64], P('mdl'), may hold values from 0.5 to 2
- conv_inner: float32 [4, 4096], P(None, 'mdl'), may hold values from -3 to 3
- conv_state: float32 [4, 256], replicated, may hold values from -3 to 3
- norm_gain: float32 [4096], P('mdl'), may hold values from 0.1 to 1.9
- out_weight: bfloat16 [4096, 2048], P('mdl', 'req'), may hold values from -0.09375 to 0.09375
- state_pool: float32 [512, 64, 64, 128], P('req', 'mdl'), may hold values from -2.4 to 2.4
- conv_pool_inner: bfloat16 [512, 3, 4096], P('req', None, 'mdl'), may hold values from -6 to 6
- conv_pool_state: bfloat16 [512, 3, 256], P('req'), may hold values from -6 to 6
- owner_dev: int32 [512], replicated, may hold values from 0 to 63, as said below
- state_page: int32 [512], replicated, may hold values from 0 to 7, as said below
- conv_page: int32 [512], replicated, may hold values from 0 to 7, as said below
- accepted: int32 [512], replicated, may hold values from 1 to 16
Outputs:
- mixed: bfloat16 [8192, 2048], P('req', 'mdl')
- new_states: float32 [512, 64, 64, 128], P('req', 'mdl')
- conv_inner_out: bfloat16 [512, 3, 4096], P('req', None, 'mdl')
- conv_state_out: bfloat16 [512, 3, 256], P('req')
Inputs may be any that keep to these rules, and one draw needn't show every extreme that they name: `owner_dev`: request r of device i = r // 8 has its owner among devices i to i + 7 along req, counted modulo the axis size; among the 8 requests of one device at most 2 name the same owner, and exactly 2 do for one owner; every owner is named by exactly 8 requests in all. `state_page`: the requests of one owner have distinct state slots. `conv_page`: the requests of one owner have distinct convolution pages.
All inputs are finite; a program needn't handle non-finite values.
Results may differ from a plain program's by a relative error of at most 0.0069.
Values may be sent and summed in bfloat16 or wider, within the bound.
A program may use at most 64 MiB of HBM per device.

v0:
```python
import jax
import jax.numpy as jnp
from jax import lax
from jax.sharding import PartitionSpec as P

KCONV = 4
CAP = 2
WINDOW = 8
HIGH = lax.Precision.HIGHEST
EPSILON = 1e-05


def from_behind(value, axis, steps):
    count = lax.axis_size(axis)
    pairs = [(source, (source + steps) % count) for source in range(count)]
    return lax.ppermute(value, axis, pairs)


def one_hot_apply(table, values, shape):
    flat = values.reshape(table.shape[1], -1)
    return (
        jnp.dot(table, flat, preferred_element_type=jnp.float32).astype(jnp.bfloat16).reshape(shape)
    )


def route_tables(owner_dev, state_page, conv_page, accepted, groups, per_dev, this_dev):
    owner_grid = owner_dev.reshape(groups, per_dev)
    home_grid = jnp.arange(groups, dtype=jnp.int32)[:, None]
    offset_grid = (owner_grid - home_grid + groups) % groups
    positions = jnp.arange(per_dev, dtype=jnp.int32)
    earlier = positions[None, :] < positions[:, None]
    pair_rank = jnp.sum((owner_grid[:, :, None] == owner_grid[:, None, :]) & earlier[None], axis=2)
    slot_grid = offset_grid * CAP + pair_rank
    send_at = lax.dynamic_slice_in_dim(slot_grid, this_dev, 1, 0)[0]
    buffer_rows = jnp.arange(WINDOW * CAP, dtype=jnp.int32)
    send_table = (buffer_rows[:, None] == send_at[None, :]).astype(jnp.bfloat16)
    arrive_at = slot_grid.reshape(-1)
    slot_match = (owner_dev[None, :] == this_dev) & (state_page[None, :] == positions[:, None])
    pick_from = jnp.sum(jnp.where(slot_match, arrive_at[None, :], 0), axis=1)
    conv_of = jnp.sum(jnp.where(slot_match, conv_page[None, :], 0), axis=1)
    kept_count = jnp.sum(jnp.where(slot_match, accepted[None, :], 0), axis=1)
    gather_table = (buffer_rows[None, :] == pick_from[:, None]).astype(jnp.bfloat16)
    place_table = (positions[:, None] == conv_of[None, :]).astype(jnp.bfloat16)
    return (send_table, gather_table, place_table, conv_of, kept_count)


def project_in(rows, z_weight, x_weight, state_proj, step_weight):
    pieces = (
        lax.all_gather(z_weight, "req", axis=0, tiled=True),
        lax.all_gather(x_weight, "req", axis=0, tiled=True),
        lax.all_gather(state_proj, "req", axis=0, tiled=True),
        lax.all_gather(step_weight, "req", axis=0, tiled=True),
    )
    gate_pre, inner_raw, state_full, step_raw = tuple(
        (jnp.dot(rows, piece, preferred_element_type=jnp.float32) for piece in pieces)
    )
    state_raw = state_full.astype(jnp.bfloat16)
    packed = jnp.concatenate([inner_raw.astype(jnp.bfloat16), state_raw], axis=1)
    return (gate_pre, packed, step_raw.astype(jnp.bfloat16))


def mix_requests(
    packed, step_raw, history, kernel, step_bias, decay_log, skip_gain, state_pool, kept_count
):
    per_dev, draft, channels = packed.shape
    heads, head_dim, state_width = (state_pool.shape[1], state_pool.shape[2], state_pool.shape[3])
    inner = heads * head_dim
    series = jnp.concatenate([history, packed], axis=1)
    series_f = series.astype(jnp.float32)
    conv_sum = kernel[0] * series_f[:, 0:draft]
    for tap in range(1, KCONV):
        conv_sum = conv_sum + kernel[tap] * series_f[:, tap : tap + draft]
    active = jax.nn.silu(conv_sum)
    inputs_x = active[:, :, :inner].reshape(per_dev, draft, heads, head_dim)
    b_rows = active[:, :, inner : inner + state_width]
    c_rows = active[:, :, inner + state_width :]
    step_size = jax.nn.softplus(step_raw.astype(jnp.float32) + step_bias)
    log_decay = jnp.cumsum(step_size * -jnp.exp(decay_log), axis=1)
    step_order = jnp.arange(draft, dtype=jnp.int32)
    causal = (step_order[None, :] <= step_order[:, None])[None, :, :, None]
    spread = log_decay[:, :, None, :] - log_decay[:, None, :, :]
    decay_table = jnp.where(causal, jnp.exp(jnp.where(causal, spread, 0.0)), 0.0)
    scores = jnp.einsum("stn,sun->stu", c_rows, b_rows, precision=HIGH)
    weights = decay_table * scores[:, :, :, None] * step_size[:, None, :, :]
    within = jnp.einsum("stuh,suhp->sthp", weights, inputs_x, precision=HIGH)
    carried = (
        jnp.einsum("stn,shpn->sthp", c_rows, state_pool, precision=HIGH)
        * jnp.exp(log_decay)[:, :, :, None]
    )
    outputs = within + carried + skip_gain[:, None] * inputs_x
    at_end = (step_order[None, :] == (kept_count - 1)[:, None])[:, :, None]
    end_decay = jnp.sum(jnp.where(at_end, log_decay, 0.0), axis=1)
    before = (step_order[None, :] < kept_count[:, None])[:, :, None]
    gap = end_decay[:, None, :] - log_decay
    select_weight = jnp.where(before, jnp.exp(jnp.where(before, gap, 0.0)), 0.0) * step_size
    chosen = jnp.exp(end_decay)[:, :, None, None] * state_pool + jnp.einsum(
        "suh,suhp,sun->shpn", select_weight, inputs_x, b_rows, precision=HIGH
    )
    series_rows = jnp.arange(series.shape[1], dtype=jnp.int32)
    window = (
        series_rows[None, None, :]
        == kept_count[:, None, None] + jnp.arange(KCONV - 1, dtype=jnp.int32)[None, :, None]
    ).astype(jnp.bfloat16)
    edge_rows = jnp.einsum(
        "sir,src->sic", window, series, preferred_element_type=jnp.float32
    ).astype(jnp.bfloat16)
    return (outputs.reshape(per_dev, draft, inner).astype(jnp.bfloat16), chosen, edge_rows)


def finish(mixed_rows, gate_pre, norm_gain, out_weight):
    gated = mixed_rows.astype(jnp.float32) * jax.nn.silu(gate_pre)
    inner_total = gated.shape[1] * lax.axis_size("mdl")
    squares = lax.psum(jnp.sum(gated * gated, axis=1), "mdl")
    normed = (gated * lax.rsqrt(squares[:, None] / inner_total + EPSILON) * norm_gain).astype(
        jnp.bfloat16
    )
    terms = jnp.dot(
        normed,
        lax.all_gather(out_weight, "req", axis=1, tiled=True),
        preferred_element_type=jnp.float32,
    )
    return lax.psum_scatter(terms, "mdl", scatter_dimension=1, tiled=True).astype(jnp.bfloat16)


def on_device(
    hidden_in,
    z_weight,
    x_weight,
    state_proj,
    step_weight,
    step_bias,
    decay_log,
    skip_gain,
    conv_inner,
    conv_state,
    norm_gain,
    out_weight,
    state_pool,
    conv_pool_inner,
    conv_pool_state,
    owner_dev,
    state_page,
    conv_page,
    accepted,
):
    groups = lax.axis_size("req")
    this_dev = lax.axis_index("req")
    per_dev = state_pool.shape[0]
    draft = hidden_in.shape[0] // per_dev
    slots = WINDOW * CAP
    send_table, gather_table, place_table, conv_of, kept_count = route_tables(
        owner_dev, state_page, conv_page, accepted, groups, per_dev, this_dev
    )
    history = jnp.concatenate([conv_pool_inner[conv_of], conv_pool_state[conv_of]], axis=2)
    kernel = jnp.concatenate([conv_inner, conv_state], axis=1)
    gate_pre, packed, step_raw = project_in(hidden_in, z_weight, x_weight, state_proj, step_weight)
    channels = packed.shape[1]
    payload = jnp.concatenate([packed, step_raw], axis=1)
    total_cols = payload.shape[1]
    outgoing = one_hot_apply(send_table, payload, (slots, draft, total_cols))
    incoming = jnp.concatenate(
        [
            from_behind(outgoing[offset * CAP : (offset + 1) * CAP], "req", offset)
            for offset in range(WINDOW)
        ],
        axis=0,
    )
    owned = one_hot_apply(gather_table, incoming, (per_dev, draft, total_cols))
    mixed_rows, chosen, edge_rows = mix_requests(
        owned[:, :, :channels],
        owned[:, :, channels:],
        history,
        kernel,
        step_bias,
        decay_log,
        skip_gain,
        state_pool,
        kept_count,
    )
    inner_local = mixed_rows.shape[2]
    returning = one_hot_apply(gather_table.T, mixed_rows, (slots, draft, inner_local))
    arrived = jnp.concatenate(
        [
            from_behind(returning[offset * CAP : (offset + 1) * CAP], "req", -offset)
            for offset in range(WINDOW)
        ],
        axis=0,
    )
    home_rows = one_hot_apply(send_table.T, arrived, (per_dev * draft, inner_local))
    mixed = finish(home_rows, gate_pre, norm_gain, out_weight)
    placed = one_hot_apply(place_table, edge_rows, edge_rows.shape)
    inner_cols = conv_pool_inner.shape[2]
    return (mixed, chosen, placed[:, :, :inner_cols], placed[:, :, inner_cols:])


def solution(mesh):
    return jax.shard_map(
        on_device,
        mesh=mesh,
        in_specs=(
            P("req", None),
            P("req", "mdl"),
            P("req", "mdl"),
            P("req", None),
            P("req", "mdl"),
            P("mdl"),
            P("mdl"),
            P("mdl"),
            P(None, "mdl"),
            P(),
            P("mdl"),
            P("mdl", "req"),
            P("req", "mdl", None, None),
            P("req", None, "mdl"),
            P("req", None, None),
            P(),
            P(),
            P(),
            P(),
        ),
        out_specs=(
            P("req", "mdl"),
            P("req", "mdl", None, None),
            P("req", None, "mdl"),
            P("req", None, None),
        ),
        check_vma=False,
    )
```

profile of v0, /device:TPU:4, one launch (start us, length us, event | category | flops | bytes accessed | tf_op | source)
XLA Modules:
  0.0 400.5 jit_solution(18413724058797244592)
XLA Ops:
  10.0 0.8 reshape.219
  12.7 0.9 select_reduce_fusion.1
  14.8 55.4 %all-gather = bf16[64,32,8]{1,2,0:T(8,128)(2,1)S(1)} all-gather(bf16[1,32,8]{1,2,0:T(8,128)(2,1)} %bitcast.102), channel_id=1, replica_groups=mesh['req'=64,'mdl'=8] {'req'}, dimensions={0}, use_global_device_ids=true | all-gather | bytes 33280 | tf_op jit(solution)/shard_map/all_gather | solution.py:52
  73.0 24.6 %all-gather.8.cloned.1.call-done = bf16[2048,256]{1,0:T(8,128)(2,1)} async-done(((bf16[32,256]{1,0:T(8,128)(2,1)}), bf16[2048,256]{1,0:T(8,128)(2,1)}) %all-gather.8.cloned.1.call-update) | async-done | bytes 1048592 | tf_op jit(solution)/shard_map/all_gather | solution.py:51
  97.6 1.5 convolution_convert_fusion.6
  99.2 82.5 %all-gather.6.cloned.1.call-done = bf16[2048,512]{1,0:T(8,128)(2,1)} async-done(((bf16[32,512]{1,0:T(8,128)(2,1)}), bf16[2048,512]{1,0:T(8,128)(2,1)}) %all-gather.6.cloned.1.call-update) | async-done | bytes 2097168 | tf_op jit(solution)/shard_map/all_gather | solution.py:50
  181.7 2.0 convolution_convert_fusion.5
  186.8 2.2 collective-permute-start.1
  189.2 3.1 collective-permute-start.2
  192.4 3.3 collective-permute-start.3
  195.9 3.3 collective-permute-start.4
  199.7 4.5 %collective-permute-start.5 = (bf16[2,16,776]{2,1,0:T(8,128)(2,1)S(1)}, bf16[2,16,776]{2,1,0:T(8,128)(2,1)S(1)}, u32[]{:S(2)}, u32[]{:S(2)}) collective-permute-start(bf16[2,16,776]{2,1,0:T(8,128)(2,1)S(1)} %slice.153), channel_id=1, source_target_pairs={{0,40},{8,48},{16,56},{24,64},{32,72},{40,80},{48,88},{56,96},{64,... | collective-permute-start | bytes 149000 | tf_op jit(solution)/shard_map/ppermute | solution.py:16
  204.2 4.1 %collective-permute-start.6 = (bf16[2,16,776]{2,1,0:T(8,128)(2,1)S(1)}, bf16[2,16,776]{2,1,0:T(8,128)(2,1)S(1)}, u32[]{:S(2)}, u32[]{:S(2)}) collective-permute-start(bf16[2,16,776]{2,1,0:T(8,128)(2,1)S(1)} %slice.155), channel_id=1, source_target_pairs={{0,48},{8,56},{16,64},{24,72},{32,80},{40,88},{48,96},{56,104},{64... | collective-permute-start | bytes 149000 | tf_op jit(solution)/shard_map/ppermute | solution.py:16
  208.3 3.9 collective-permute-start.7
  212.4 2.6 collective-permute-done.7
  218.2 0.7 slice.209
  218.9 0.9 fusion.29
  220.4 1.1 reshape.223
  221.6 5.8 %convolution_multiply_fusion = f32[8,16,8,64]{3,1,2,0:T(8,128)S(1)} fusion(f32[8,8,64,128]{3,2,1,0:T(8,128)S(1)} %copy-done.1, f32[8,16,8]{1,2,0:T(8,128)} %copy.138, f32[8,16,768]{2,1,0:T(8,128)S(1)} %divide_multiply_fusion), kind=kOutput, calls=%fused_computation.9 | convolution fusion | flops 100728832 | bytes 2428928 | tf_op jit(solution)/shard_map/stn,shpn->sthp/dot_general | solution.py:87
  228.2 0.9 fusion.3
  229.1 0.8 copy.140
  229.9 1.9 convert_element_type.68
  231.7 1.2 convolution_convert_fusion.2
  233.2 3.8 collective-permute-start.9
  237.0 2.1 collective-permute-start.10
  239.2 2.8 collective-permute-start.11
  241.9 4.8 %collective-permute-start.12 = (bf16[2,16,512]{2,1,0:T(8,128)(2,1)S(1)}, bf16[2,16,512]{2,1,0:T(8,128)(2,1)S(1)}, u32[]{:S(2)}, u32[]{:S(2)}) collective-permute-start(bf16[2,16,512]{2,1,0:T(8,128)(2,1)S(1)} %bitcast.97), channel_id=1, source_target_pairs={{0,480},{8,488},{16,496},{24,504},{32,0},{40,8},{48,16},{56,24},{6... | collective-permute-start | bytes 98312 | tf_op jit(solution)/shard_map/ppermute | solution.py:16
  246.8 2.4 collective-permute-start.13
  249.2 4.7 %collective-permute-start.14 = (bf16[2,16,512]{2,1,0:T(8,128)(2,1)S(1)}, bf16[2,16,512]{2,1,0:T(8,128)(2,1)S(1)}, u32[]{:S(2)}, u32[]{:S(2)}) collective-permute-start(bf16[2,16,512]{2,1,0:T(8,128)(2,1)S(1)} %bitcast.95), channel_id=1, source_target_pairs={{0,464},{8,472},{16,480},{24,488},{32,496},{40,504},{48,0},{56,8},... | collective-permute-start | bytes 98312 | tf_op jit(solution)/shard_map/ppermute | solution.py:16
  253.9 1.9 collective-permute-start.15
  255.9 0.7 collective-permute-done.14
  256.7 3.4 collective-permute-done.15
  260.2 0.9 fusion
  261.2 1.7 reshape.227
  262.9 2.7 all-gather.10.cloned.1.call-done
  265.6 2.7 multiply_reduce_fusion
  268.4 17.2 %psum.7 = f32[128]{0:T(128)S(1)} all-reduce(f32[128]{0:T(128)S(1)} %get-tuple-element.29), channel_id=1, replica_groups=mesh['req'=64,'mdl'=8] {'mdl'}, use_global_device_ids=true, to_apply=%region_5.6 | all-reduce | flops 128 | bytes 1024 | tf_op jit(solution)/shard_map/psum | solution.py:113
  286.1 63.5 %all-gather.12.cloned.1.call-done = bf16[512,2048]{0,1:T(8,128)(2,1)} async-done(((bf16[512,32]{0,1:T(8,128)(2,1)}), bf16[512,2048]{0,1:T(8,128)(2,1)}) %all-gather.12.cloned.1.call-update) | async-done | bytes 2097168 | tf_op jit(solution)/shard_map/all_gather | solution.py:119
  349.6 3.6 fusion.23
  353.2 0.7 iota_add_fusion
  353.9 1.3 exp.41
  355.2 1.2 fusion.4
  356.4 0.7 convolution_convert_fusion.4
  358.3 1.5 copy.143
  359.8 1.0 broadcast_multiply_fusion
  360.8 5.6 %multiply_add_fusion = f32[8,8,64,128]{3,2,1,0:T(8,128)} fusion(f32[8,8,64,128]{3,2,1,0:T(8,128)S(1)} %copy-done.1, f32[8,8]{1,0:T(8,128)} %exp.41, f32[8,16,8,64]{3,2,1,0:T(8,128)S(1)} %broadcast_multiply_fusion, f32[8,16,768]{2,1,0:T(8,128)S(1)} %divide_multiply_fusion), kind=kOutput, calls=%fused_computation.8 | convolution fusion | flops 101711872 | bytes 4784384 | tf_op jit(solution)/shard_map/suh,suhp,sun->shpn/dot_general | solution.py:96
  366.5 26.0 %reduce-scatter.2.cloned.1.call-done = f32[128,256]{1,0:T(8,128)} async-done(((f32[128,2048]{1,0:T(8,128)}), f32[128,256]{1,0:T(8,128)}) %reduce-scatter.2.cloned.1.call-update) | async-done | bytes 131088 | tf_op jit(solution)/shard_map/reduce_scatter | solution.py:122
  392.4 1.5 convert_element_type.74
  (156 shorter events, 19.7 us)
Async XLA Ops:
  7.2 63.2 %copy-start = (bf16[128,2048]{1,0:T(8,128)(2,1)S(1)}, bf16[128,2048]{1,0:T(8,128)(2,1)}, u32[]{:S(2)}) copy-start(bf16[128,2048]{1,0:T(8,128)(2,1)} %param.19) | copy-start | bytes 1572868
  7.2 90.4 %all-gather.8.cloned.1.call-start = ((), (), s32[]{:S(2)}) async-start(), calls=%async_computation.2 | async-start | bytes 1064960 | tf_op jit(solution)/shard_map/all_gather | solution.py:51
  7.9 173.8 %all-gather.6.cloned.1.call-start = ((), (), s32[]{:S(2)}) async-start(), calls=%async_computation.1 | async-start | bytes 2129920 | tf_op jit(solution)/shard_map/all_gather | solution.py:50
  8.7 256.9 %all-gather.10.cloned.1.call-start = ((), (), s32[]{:S(2)}) async-start(), calls=%async_computation.3 | async-start | bytes 2129920 | tf_op jit(solution)/shard_map/all_gather | solution.py:49
  9.4 340.2 %all-gather.12.cloned.1.call-start = ((), (), s32[]{:S(2)}) async-start(), calls=%async_computation.4 | async-start | bytes 2129920 | tf_op jit(solution)/shard_map/all_gather | solution.py:119
  10.0 382.5 %reduce-scatter.2.cloned.1.call-start = ((), (), s32[]{:S(2)}) async-start(), calls=%async_computation.5 | async-start | bytes 1179648 | tf_op jit(solution)/shard_map/reduce_scatter | solution.py:122
  13.5 168.2 %copy-start.16 = (s32[8]{0:T(128)}, s32[8]{0:T(128)S(1)}, u32[]{:S(2)}) copy-start(s32[8]{0:T(128)S(1)} %get-tuple-element.9) | copy-start | bytes 100
  13.5 168.1 %copy-start.17 = (s32[8]{0:T(128)}, s32[8]{0:T(128)S(1)}, u32[]{:S(2)}) copy-start(s32[8]{0:T(128)S(1)} %get-tuple-element.8) | copy-start | bytes 100
  13.5 202.0 %copy-start.13 = (s32[8]{0:T(128)}, s32[8]{0:T(128)S(1)}, u32[]{:S(2)}) copy-start(s32[8]{0:T(128)S(1)} %get-tuple-element.10) | copy-start | bytes 100
  73.0 111.0 %copy-start.11 = (s32[8]{0:T(128)}, s32[8]{0:T(128)S(1)}, u32[]{:S(2)}) copy-start(s32[8]{0:T(128)S(1)} %dynamic-slice_reduce_fusion) | copy-start | bytes 100
  99.2 86.2 %copy-start.3 = (bf16[8,3,256]{2,0,1:T(8,128)(2,1)S(1)}, bf16[8,3,256]{2,0,1:T(8,128)(2,1)}, u32[]{:S(2)}) copy-start(bf16[8,3,256]{2,0,1:T(8,128)(2,1)} %param.33) | copy-start | bytes 36868
  99.2 86.8 %copy-start.2 = (bf16[8,3,512]{2,0,1:T(8,128)(2,1)S(1)}, bf16[8,3,512]{2,0,1:T(8,128)(2,1)}, u32[]{:S(2)}) copy-start(bf16[8,3,512]{2,0,1:T(8,128)(2,1)} %param.32) | copy-start | bytes 73732
  184.7 15.0 %collective-permute-start = (bf16[2,16,776]{2,1,0:T(8,128)(2,1)S(1)}, bf16[2,16,776]{2,1,0:T(8,128)(2,1)S(1)}, u32[]{:S(2)}, u32[]{:S(2)}) collective-permute-start(bf16[2,16,776]{2,1,0:T(8,128)(2,1)S(1)} %slice.143), channel_id=1, source_target_pairs={{0,0},{8,8},{16,16},{24,24},{32,32},{40,40},{48,48},{56,56},{64,64... | collective-permute-start | bytes 149000 | tf_op jit(solution)/shard_map/ppermute | solution.py:16
  186.0 31.9 %copy-start.8 = (bf16[8,3,256]{2,1,0:T(4,128)(2,1)}, bf16[8,3,256]{2,1,0:T(4,128)(2,1)S(1)}, u32[]{:S(2)}) copy-start(bf16[8,3,256]{2,1,0:T(4,128)(2,1)S(1)} %copy.130) | copy-start | bytes 36868
  186.6 29.6 %copy-start.14 = (f32[8]{0:T(128)S(1)}, f32[8]{0:T(128)}, u32[]{:S(2)}) copy-start(f32[8]{0:T(128)} %param.24) | copy-start | bytes 100
  186.6 31.2 %copy-start.6 = (bf16[8,3,512]{2,1,0:T(4,128)(2,1)}, bf16[8,3,512]{2,1,0:T(4,128)(2,1)S(1)}, u32[]{:S(2)}) copy-start(bf16[8,3,512]{2,1,0:T(4,128)(2,1)S(1)} %copy.129) | copy-start | bytes 73732
  186.8 17.4 %collective-permute-start.1 = (bf16[2,16,776]{2,1,0:T(8,128)(2,1)S(1)}, bf16[2,16,776]{2,1,0:T(8,128)(2,1)S(1)}, u32[]{:S(2)}, u32[]{:S(2)}) collective-permute-start(bf16[2,16,776]{2,1,0:T(8,128)(2,1)S(1)} %slice.145), channel_id=1, source_target_pairs={{0,8},{8,16},{16,24},{24,32},{32,40},{40,48},{48,56},{56,64},{64,7... | collective-permute-start | bytes 149000 | tf_op jit(solution)/shard_map/ppermute | solution.py:16
  189.2 19.1 %collective-permute-start.2 = (bf16[2,16,776]{2,1,0:T(8,128)(2,1)S(1)}, bf16[2,16,776]{2,1,0:T(8,128)(2,1)S(1)}, u32[]{:S(2)}, u32[]{:S(2)}) collective-permute-start(bf16[2,16,776]{2,1,0:T(8,128)(2,1)S(1)} %slice.147), channel_id=1, source_target_pairs={{0,16},{8,24},{16,32},{24,40},{32,48},{40,56},{48,64},{56,72},{64,... | collective-permute-start | bytes 149000 | tf_op jit(solution)/shard_map/ppermute | solution.py:16
  192.4 19.8 %collective-permute-start.3 = (bf16[2,16,776]{2,1,0:T(8,128)(2,1)S(1)}, bf16[2,16,776]{2,1,0:T(8,128)(2,1)S(1)}, u32[]{:S(2)}, u32[]{:S(2)}) collective-permute-start(bf16[2,16,776]{2,1,0:T(8,128)(2,1)S(1)} %slice.149), channel_id=1, source_target_pairs={{0,24},{8,32},{16,40},{24,48},{32,56},{40,64},{48,72},{56,80},{64,... | collective-permute-start | bytes 149000 | tf_op jit(solution)/shard_map/ppermute | solution.py:16
  195.9 16.4 %collective-permute-start.4 = (bf16[2,16,776]{2,1,0:T(8,128)(2,1)S(1)}, bf16[2,16,776]{2,1,0:T(8,128)(2,1)S(1)}, u32[]{:S(2)}, u32[]{:S(2)}) collective-permute-start(bf16[2,16,776]{2,1,0:T(8,128)(2,1)S(1)} %slice.151), channel_id=1, source_target_pairs={{0,32},{8,40},{16,48},{24,56},{32,64},{40,72},{48,80},{56,88},{64,... | collective-permute-start | bytes 149000 | tf_op jit(solution)/shard_map/ppermute | solution.py:16
  199.7 12.6 %collective-permute-start.5 = (bf16[2,16,776]{2,1,0:T(8,128)(2,1)S(1)}, bf16[2,16,776]{2,1,0:T(8,128)(2,1)S(1)}, u32[]{:S(2)}, u32[]{:S(2)}) collective-permute-start(bf16[2,16,776]{2,1,0:T(8,128)(2,1)S(1)} %slice.153), channel_id=1, source_target_pairs={{0,40},{8,48},{16,56},{24,64},{32,72},{40,80},{48,88},{56,96},{64,... | collective-permute-start | bytes 149000 | tf_op jit(solution)/shard_map/ppermute | solution.py:16
  204.2 8.2 %collective-permute-start.6 = (bf16[2,16,776]{2,1,0:T(8,128)(2,1)S(1)}, bf16[2,16,776]{2,1,0:T(8,128)(2,1)S(1)}, u32[]{:S(2)}, u32[]{:S(2)}) collective-permute-start(bf16[2,16,776]{2,1,0:T(8,128)(2,1)S(1)} %slice.155), channel_id=1, source_target_pairs={{0,48},{8,56},{16,64},{24,72},{32,80},{40,88},{48,96},{56,104},{64... | collective-permute-start | bytes 149000 | tf_op jit(solution)/shard_map/ppermute | solution.py:16
  208.3 6.7 %collective-permute-start.7 = (bf16[2,16,776]{2,1,0:T(8,128)(2,1)S(1)}, bf16[2,16,776]{2,1,0:T(8,128)(2,1)S(1)}, u32[]{:S(2)}, u32[]{:S(2)}) collective-permute-start(bf16[2,16,776]{2,1,0:T(8,128)(2,1)S(1)} %slice.157), channel_id=1, source_target_pairs={{0,56},{8,64},{16,72},{24,80},{32,88},{40,96},{48,104},{56,112},{6... | collective-permute-start | bytes 149000 | tf_op jit(solution)/shard_map/ppermute | solution.py:16
  216.1 1.8 copy-start.4
  217.8 3.7 copy-start.1
  221.5 5.8 %copy-start.5 = (f32[8,16,8]{1,2,0:T(8,128)S(1)}, f32[8,16,8]{1,2,0:T(8,128)}, u32[]{:S(2)}) copy-start(f32[8,16,8]{1,2,0:T(8,128)} %copy.135) | copy-start | bytes 12292
  221.5 5.8 %copy-start.20 = (pred[8,16]{1,0:T(8,128)(4,1)S(1)}, pred[8,16]{1,0:T(8,128)(4,1)}, u32[]{:S(2)}) copy-start(pred[8,16]{1,0:T(8,128)(4,1)} %iota_compare_fusion.9) | copy-start | bytes 388
  221.5 5.9 %copy-start.15 = (f32[8]{0:T(128)S(1)}, f32[8]{0:T(128)}, u32[]{:S(2)}) copy-start(f32[8]{0:T(128)} %param.24) | copy-start | bytes 100
  221.6 5.9 %copy-start.19 = (pred[8,16]{1,0:T(8,128)(4,1)S(1)}, pred[8,16]{1,0:T(8,128)(4,1)}, u32[]{:S(2)}) copy-start(pred[8,16]{1,0:T(8,128)(4,1)} %iota_compare_fusion.8) | copy-start | bytes 388
  221.6 6.6 %copy-start.7 = (f32[8,16,16]{2,1,0:T(8,128)S(1)}, f32[8,16,16]{2,1,0:T(8,128)}, u32[]{:S(2)}) copy-start(f32[8,16,16]{2,1,0:T(8,128)} %fusion.29) | copy-start | bytes 24580
  221.6 6.6 %copy-start.18 = (pred[16,16]{1,0:T(8,128)(4,1)S(1)}, pred[16,16]{1,0:T(8,128)(4,1)}, u32[]{:S(2)}) copy-start(pred[16,16]{1,0:T(8,128)(4,1)} %iota_compare_fusion.3) | copy-start | bytes 772
  221.6 6.6 %copy-start.21 = (f32[8]{0:T(128)S(1)}, f32[8]{0:T(128)}, u32[]{:S(2)}) copy-start(f32[8]{0:T(128)} %param.26) | copy-start | bytes 100
  227.5 0.7 copy-start.10
  229.1 31.1 %copy-start.12 = (s32[8]{0:T(128)S(1)}, s32[8]{0:T(128)}, u32[]{:S(2)}) copy-start(s32[8]{0:T(128)} %copy-done.11) | copy-start | bytes 100
  233.2 13.6 %collective-permute-start.8 = (bf16[2,16,512]{2,1,0:T(8,128)(2,1)S(1)}, bf16[2,16,512]{2,1,0:T(8,128)(2,1)S(1)}, u32[]{:S(2)}, u32[]{:S(2)}) collective-permute-start(bf16[2,16,512]{2,1,0:T(8,128)(2,1)S(1)} %bitcast.101), channel_id=1, source_target_pairs={{0,0},{8,8},{16,16},{24,24},{32,32},{40,40},{48,48},{56,56},{64,64... | collective-permute-start | bytes 98312 | tf_op jit(solution)/shard_map/ppermute | solution.py:16
  233.2 16.0 %collective-permute-start.9 = (bf16[2,16,512]{2,1,0:T(8,128)(2,1)S(1)}, bf16[2,16,512]{2,1,0:T(8,128)(2,1)S(1)}, u32[]{:S(2)}, u32[]{:S(2)}) collective-permute-start(bf16[2,16,512]{2,1,0:T(8,128)(2,1)S(1)} %bitcast.100), channel_id=1, source_target_pairs={{0,504},{8,0},{16,8},{24,16},{32,24},{40,32},{48,40},{56,48},{64,5... | collective-permute-start | bytes 98312 | tf_op jit(solution)/shard_map/ppermute | solution.py:16
  237.0 16.9 %collective-permute-start.10 = (bf16[2,16,512]{2,1,0:T(8,128)(2,1)S(1)}, bf16[2,16,512]{2,1,0:T(8,128)(2,1)S(1)}, u32[]{:S(2)}, u32[]{:S(2)}) collective-permute-start(bf16[2,16,512]{2,1,0:T(8,128)(2,1)S(1)} %bitcast.99), channel_id=1, source_target_pairs={{0,496},{8,504},{16,0},{24,8},{32,16},{40,24},{48,32},{56,40},{64,... | collective-permute-start | bytes 98312 | tf_op jit(solution)/shard_map/ppermute | solution.py:16
  239.2 16.7 %collective-permute-start.11 = (bf16[2,16,512]{2,1,0:T(8,128)(2,1)S(1)}, bf16[2,16,512]{2,1,0:T(8,128)(2,1)S(1)}, u32[]{:S(2)}, u32[]{:S(2)}) collective-permute-start(bf16[2,16,512]{2,1,0:T(8,128)(2,1)S(1)} %bitcast.98), channel_id=1, source_target_pairs={{0,488},{8,496},{16,504},{24,0},{32,8},{40,16},{48,24},{56,32},{64... | collective-permute-start | bytes 98312 | tf_op jit(solution)/shard_map/ppermute | solution.py:16
  241.9 13.9 %collective-permute-start.12 = (bf16[2,16,512]{2,1,0:T(8,128)(2,1)S(1)}, bf16[2,16,512]{2,1,0:T(8,128)(2,1)S(1)}, u32[]{:S(2)}, u32[]{:S(2)}) collective-permute-start(bf16[2,16,512]{2,1,0:T(8,128)(2,1)S(1)} %bitcast.97), channel_id=1, source_target_pairs={{0,480},{8,488},{16,496},{24,504},{32,0},{40,8},{48,16},{56,24},{6... | collective-permute-start | bytes 98312 | tf_op jit(solution)/shard_map/ppermute | solution.py:16
  246.8 9.1 %collective-permute-start.13 = (bf16[2,16,512]{2,1,0:T(8,128)(2,1)S(1)}, bf16[2,16,512]{2,1,0:T(8,128)(2,1)S(1)}, u32[]{:S(2)}, u32[]{:S(2)}) collective-permute-start(bf16[2,16,512]{2,1,0:T(8,128)(2,1)S(1)} %bitcast.96), channel_id=1, source_target_pairs={{0,472},{8,480},{16,488},{24,496},{32,504},{40,0},{48,8},{56,16},{... | collective-permute-start | bytes 98312 | tf_op jit(solution)/shard_map/ppermute | solution.py:16
  249.2 7.4 %collective-permute-start.14 = (bf16[2,16,512]{2,1,0:T(8,128)(2,1)S(1)}, bf16[2,16,512]{2,1,0:T(8,128)(2,1)S(1)}, u32[]{:S(2)}, u32[]{:S(2)}) collective-permute-start(bf16[2,16,512]{2,1,0:T(8,128)(2,1)S(1)} %bitcast.95), channel_id=1, source_target_pairs={{0,464},{8,472},{16,480},{24,488},{32,496},{40,504},{48,0},{56,8},... | collective-permute-start | bytes 98312 | tf_op jit(solution)/shard_map/ppermute | solution.py:16
  253.9 6.1 %collective-permute-start.15 = (bf16[2,16,512]{2,1,0:T(8,128)(2,1)S(1)}, bf16[2,16,512]{2,1,0:T(8,128)(2,1)S(1)}, u32[]{:S(2)}, u32[]{:S(2)}) collective-permute-start(bf16[2,16,512]{2,1,0:T(8,128)(2,1)S(1)} %bitcast.94), channel_id=1, source_target_pairs={{0,456},{8,464},{16,472},{24,480},{32,488},{40,496},{48,504},{56,0... | collective-permute-start | bytes 98312 | tf_op jit(solution)/shard_map/ppermute | solution.py:16
  349.6 5.6 %copy-start.9 = (bf16[8,3,256]{2,1,0:T(4,128)(2,1)S(1)}, bf16[8,3,256]{2,1,0:T(4,128)(2,1)}, u32[]{:S(2)}) copy-start(bf16[8,3,256]{2,1,0:T(4,128)(2,1)} %copy-done.8) | copy-start | bytes 36868
Sparse Core Ops, SparseCore 0:
  11.4 86.2 all-gather.7
  101.0 80.6 all-gather.5
  185.0 80.5 all-gather.9
  268.8 80.7 all-gather.11
  353.3 39.1 reduce-scatter.1
where the time goes:
time: 402 us; the launch traced here: 401 us
  waiting for transfers between devices  209 us (52%)
  blocking collectives  72.5 us (18%)
  starting transfers between devices  46.9 us (12%)
  matrix products  27.8 us (7%)
  local copies, waits for them, and re-layouts  19.2 us (5%)
  between operations  14.7 us (4%)
  other arithmetic  10.6 us (3%)
    all_gather x1, waiting for transfers between devices, project_in(): lax.all_gather(x_weight, 'req', axis=0, tiled=True)  82.5 us
    all_gather x1, waiting for transfers between devices, finish(): lax.all_gather(out_weight, 'req', axis=1, tiled=True)  63.5 us
    all_gather x1, blocking collectives, project_in(): lax.all_gather(step_weight, 'req', axis=0, tiled=True)  55.4 us
    ppermute x16, starting transfers between devices, from_behind(): return lax.ppermute(value, axis, pairs)  46.7 us
    reduce_scatter x1, waiting for transfers between devices, finish(): lax.psum_scatter(terms, 'mdl', scatter_dimension=1, tiled=True)  26 us
    all_gather x1, waiting for transfers between devices, project_in(): lax.all_gather(state_proj, 'req', axis=0, tiled=True)  24.6 us
    psum x1, blocking collectives, finish(): squares = lax.psum(jnp.sum(gated * gated, axis=1), 'mdl')  17.2 us
  transfers between devices with their start and end apart: 21, of which 9 were waited for; matrix products, arithmetic and copies ran while one was open for 13% of the time, Pallas kernels for 0%

commit v1 on v0

--- a/solution.py
+++ b/solution.py
@@ -45,11 +45,20 @@
 
 
 def project_in(rows, z_weight, x_weight, state_proj, step_weight):
+
+    def streams_form(mesh_ax, m):
+        return jnp.concatenate(
+            lax.all_to_all(
+                jnp.stack(tuple((m for _ in range(lax.axis_size(mesh_ax))))), mesh_ax, 0, 0
+            ),
+            axis=0,
+        )
+
     pieces = (
         lax.all_gather(z_weight, "req", axis=0, tiled=True),
         lax.all_gather(x_weight, "req", axis=0, tiled=True),
         lax.all_gather(state_proj, "req", axis=0, tiled=True),
-        lax.all_gather(step_weight, "req", axis=0, tiled=True),
+        streams_form("req", step_weight),
     )
     gate_pre, inner_raw, state_full, step_raw = tuple(
         (jnp.dot(rows, piece, preferred_element_type=jnp.float32) for piece in pieces)

time: 402 us -> 402 us (level)
  the two profiles are of different devices: /device:TPU:4 before, /device:TPU:6 now
where the time goes in v1:
time: 402 us; the launch traced here: 400 us
  waiting for transfers between devices  249 us (62%)
  starting transfers between devices  60.6 us (15%)
  matrix products  27.9 us (7%)
  local copies, waits for them, and re-layouts  20.8 us (5%)
  blocking collectives  17.2 us (4%)
  between operations  14.7 us (4%)
  other arithmetic  10.6 us (3%)
    all_gather x1, waiting for transfers between devices, project_in(): lax.all_gather(x_weight, 'req', axis=0, tiled=True)  82.5 us
    all_gather x1, waiting for transfers between devices, project_in(): lax.all_gather(state_proj, 'req', axis=0, tiled=True)  64.5 us
    all_gather x1, waiting for transfers between devices, finish(): lax.all_gather(out_weight, 'req', axis=1, tiled=True)  63.4 us
    ppermute x16, starting transfers between devices, from_behind(): return lax.ppermute(value, axis, pairs)  46.6 us
    reduce_scatter x1, waiting for transfers between devices, finish(): lax.psum_scatter(terms, 'mdl', scatter_dimension=1, tiled=True)  26 us
    psum x1, blocking collectives, finish(): squares = lax.psum(jnp.sum(gated * gated, axis=1), 'mdl')  17.2 us
    all_to_all x1, starting transfers between devices, streams_form(): lax.all_to_all(jnp.stack(tuple((m for _ in range(lax.axis_size(mesh_ax)))...  13.8 us
  transfers between devices with their start and end apart: 22, of which 10 were waited for; matrix products, arithmetic and copies ran while one was open for 13% of the time, Pallas kernels for 0%

profile of v1, /device:TPU:6, one launch (start us, length us, event | category | flops | bytes accessed | tf_op | source)
XLA Modules:
  0.0 400.5 jit_solution(4620947415834880086)
XLA Ops:
  10.1 0.7 reshape.257
  10.8 13.8 %all-to-all-start = ((bf16[64,2,128]{2,1,0:T(2,128)(2,1)}), bf16[64,2,128]{2,1,0:T(2,128)(2,1)S(1)}, u32[]{:S(2)}, u32[]{:S(2)}) async-start(bf16[64,2,128]{2,1,0:T(2,128)(2,1)} %reshape.257), calls=%async_computation | async-start | bytes 65536 | tf_op jit(solution)/shard_map/all_to_all | solution.py:51
  25.3 0.8 reshape.224
  27.9 0.9 select_reduce_fusion.1
  33.2 64.5 %all-gather.7.cloned.1.call-done = bf16[2048,256]{1,0:T(8,128)(2,1)} async-done(((bf16[32,256]{1,0:T(8,128)(2,1)}), bf16[2048,256]{1,0:T(8,128)(2,1)}) %all-gather.7.cloned.1.call-update) | async-done | bytes 1048592 | tf_op jit(solution)/shard_map/all_gather | solution.py:60
  97.6 1.5 convolution_convert_fusion.6
  99.2 82.5 %all-gather.5.cloned.1.call-done = bf16[2048,512]{1,0:T(8,128)(2,1)} async-done(((bf16[32,512]{1,0:T(8,128)(2,1)}), bf16[2048,512]{1,0:T(8,128)(2,1)}) %all-gather.5.cloned.1.call-update) | async-done | bytes 2097168 | tf_op jit(solution)/shard_map/all_gather | solution.py:59
  181.6 2.0 convolution_convert_fusion.5
  186.8 2.2 collective-permute-start.1
  189.1 3.4 collective-permute-start.2
  192.7 3.3 collective-permute-start.3
  196.2 5.2 %collective-permute-start.4 = (bf16[2,16,776]{2,1,0:T(8,128)(2,1)S(1)}, bf16[2,16,776]{2,1,0:T(8,128)(2,1)S(1)}, u32[]{:S(2)}, u32[]{:S(2)}) collective-permute-start(bf16[2,16,776]{2,1,0:T(8,128)(2,1)S(1)} %slice.151), channel_id=1, source_target_pairs={{0,32},{8,40},{16,48},{24,56},{32,64},{40,72},{48,80},{56,88},{64,... | collective-permute-start | bytes 149000 | tf_op jit(solution)/shard_map/ppermute | solution.py:16
  201.9 2.3 collective-permute-start.5
  204.2 3.3 collective-permute-start.6
  207.5 3.2 collective-permute-start.7
  211.5 2.8 collective-permute-done.7
  217.5 0.7 slice.209
  218.2 0.9 fusion.29
  219.7 1.1 reshape.229
  220.9 5.8 %convolution_multiply_fusion = f32[8,16,8,64]{3,1,2,0:T(8,128)S(1)} fusion(f32[8,8,64,128]{3,2,1,0:T(8,128)S(1)} %copy-done.1, f32[8,16,8]{1,2,0:T(8,128)} %copy.153, f32[8,16,768]{2,1,0:T(8,128)S(1)} %divide_multiply_fusion), kind=kOutput, calls=%fused_computation.9 | convolution fusion | flops 100728832 | bytes 2428928 | tf_op jit(solution)/shard_map/stn,shpn->sthp/dot_general | solution.py:96
  226.8 0.7 select_multiply_fusion
  227.5 0.9 fusion.3
  228.4 0.8 copy.155
  229.2 1.9 convert_element_type.68
  231.1 1.2 convolution_convert_fusion.2
  232.6 3.6 collective-permute-start.9
  236.2 3.6 collective-permute-start.10
  239.8 2.0 collective-permute-start.11
  241.8 4.0 %collective-permute-start.12 = (bf16[2,16,512]{2,1,0:T(8,128)(2,1)S(1)}, bf16[2,16,512]{2,1,0:T(8,128)(2,1)S(1)}, u32[]{:S(2)}, u32[]{:S(2)}) collective-permute-start(bf16[2,16,512]{2,1,0:T(8,128)(2,1)S(1)} %bitcast.100), channel_id=1, source_target_pairs={{0,480},{8,488},{16,496},{24,504},{32,0},{40,8},{48,16},{56,24},{6... | collective-permute-start | bytes 98312 | tf_op jit(solution)/shard_map/ppermute | solution.py:16
  245.9 4.3 %collective-permute-start.13 = (bf16[2,16,512]{2,1,0:T(8,128)(2,1)S(1)}, bf16[2,16,512]{2,1,0:T(8,128)(2,1)S(1)}, u32[]{:S(2)}, u32[]{:S(2)}) collective-permute-start(bf16[2,16,512]{2,1,0:T(8,128)(2,1)S(1)} %bitcast.99), channel_id=1, source_target_pairs={{0,472},{8,480},{16,488},{24,496},{32,504},{40,0},{48,8},{56,16},{... | collective-permute-start | bytes 98312 | tf_op jit(solution)/shard_map/ppermute | solution.py:16
  250.3 1.9 collective-permute-start.14
  252.2 4.2 %collective-permute-start.15 = (bf16[2,16,512]{2,1,0:T(8,128)(2,1)S(1)}, bf16[2,16,512]{2,1,0:T(8,128)(2,1)S(1)}, u32[]{:S(2)}, u32[]{:S(2)}) collective-permute-start(bf16[2,16,512]{2,1,0:T(8,128)(2,1)S(1)} %bitcast.97), channel_id=1, source_target_pairs={{0,456},{8,464},{16,472},{24,480},{32,488},{40,496},{48,504},{56,0... | collective-permute-start | bytes 98312 | tf_op jit(solution)/shard_map/ppermute | solution.py:16
  257.0 1.5 collective-permute-done.15
  258.6 0.9 fusion
  259.5 1.7 reshape.233
  261.2 4.4 %all-gather.9.cloned.1.call-done = bf16[2048,512]{1,0:T(8,128)(2,1)} async-done(((bf16[32,512]{1,0:T(8,128)(2,1)}), bf16[2048,512]{1,0:T(8,128)(2,1)}) %all-gather.9.cloned.1.call-update) | async-done | bytes 2097168 | tf_op jit(solution)/shard_map/all_gather | solution.py:58
  265.7 2.8 multiply_reduce_fusion
  268.4 17.2 %psum.7 = f32[128]{0:T(128)S(1)} all-reduce(f32[128]{0:T(128)S(1)} %get-tuple-element.29), channel_id=1, replica_groups=mesh['req'=64,'mdl'=8] {'mdl'}, use_global_device_ids=true, to_apply=%region_5.6 | all-reduce | flops 128 | bytes 1024 | tf_op jit(solution)/shard_map/psum | solution.py:122
  286.1 63.4 %all-gather.11.cloned.1.call-done = bf16[512,2048]{0,1:T(8,128)(2,1)} async-done(((bf16[512,32]{0,1:T(8,128)(2,1)}), bf16[512,2048]{0,1:T(8,128)(2,1)}) %all-gather.11.cloned.1.call-update) | async-done | bytes 2097168 | tf_op jit(solution)/shard_map/all_gather | solution.py:128
  349.6 3.6 fusion.23
  353.8 1.3 exp.41
  355.1 1.2 fusion.4
  356.3 0.8 convolution_convert_fusion.4
  358.3 1.5 copy.158
  359.7 1.0 broadcast_multiply_fusion
  360.8 5.6 %multiply_add_fusion = f32[8,8,64,128]{3,2,1,0:T(8,128)} fusion(f32[8,8,64,128]{3,2,1,0:T(8,128)S(1)} %copy-done.1, f32[8,8]{1,0:T(8,128)} %exp.41, f32[8,16,8,64]{3,2,1,0:T(8,128)S(1)} %broadcast_multiply_fusion, f32[8,16,768]{2,1,0:T(8,128)S(1)} %divide_multiply_fusion), kind=kOutput, calls=%fused_computation.8 | convolution fusion | flops 101711872 | bytes 4784384 | tf_op jit(solution)/shard_map/suh,suhp,sun->shpn/dot_general | solution.py:105
  366.4 26.0 %reduce-scatter.2.cloned.1.call-done = f32[128,256]{1,0:T(8,128)} async-done(((f32[128,2048]{1,0:T(8,128)}), f32[128,256]{1,0:T(8,128)}) %reduce-scatter.2.cloned.1.call-update) | async-done | bytes 131088 | tf_op jit(solution)/shard_map/reduce_scatter | solution.py:131
  392.4 1.5 convert_element_type.74
  (160 shorter events, 21.5 us)
Async XLA Ops:
  7.2 25.6 %copy-start = (bf16[128,2048]{1,0:T(8,128)(2,1)S(1)}, bf16[128,2048]{1,0:T(8,128)(2,1)}, u32[]{:S(2)}) copy-start(bf16[128,2048]{1,0:T(8,128)(2,1)} %param.19) | copy-start | bytes 1572868
  7.2 90.4 %all-gather.7.cloned.1.call-start = ((), (), s32[]{:S(2)}) async-start(), calls=%async_computation.3 | async-start | bytes 1064960 | tf_op jit(solution)/shard_map/all_gather | solution.py:60
  7.9 173.7 %all-gather.5.cloned.1.call-start = ((), (), s32[]{:S(2)}) async-start(), calls=%async_computation.2 | async-start | bytes 2129920 | tf_op jit(solution)/shard_map/all_gather | solution.py:59
  8.7 257.0 %all-gather.9.cloned.1.call-start = ((), (), s32[]{:S(2)}) async-start(), calls=%async_computation.4 | async-start | bytes 2129920 | tf_op jit(solution)/shard_map/all_gather | solution.py:58
  10.8 21.6 %all-to-all-start = ((bf16[64,2,128]{2,1,0:T(2,128)(2,1)}), bf16[64,2,128]{2,1,0:T(2,128)(2,1)S(1)}, u32[]{:S(2)}, u32[]{:S(2)}) async-start(bf16[64,2,128]{2,1,0:T(2,128)(2,1)} %reshape.257), calls=%async_computation | async-start | bytes 65536 | tf_op jit(solution)/shard_map/all_to_all | solution.py:51
  24.7 324.9 %all-gather.11.cloned.1.call-start = ((), (), s32[]{:S(2)}) async-start(), calls=%async_computation.5 | async-start | bytes 2129920 | tf_op jit(solution)/shard_map/all_gather | solution.py:128
  25.2 367.1 %reduce-scatter.2.cloned.1.call-start = ((), (), s32[]{:S(2)}) async-start(), calls=%async_computation.6 | async-start | bytes 1179648 | tf_op jit(solution)/shard_map/reduce_scatter | solution.py:131
  28.8 3.6 copy-start.16
  28.8 3.6 copy-start.17
  28.8 186.0 %copy-start.13 = (s32[8]{0:T(128)}, s32[8]{0:T(128)S(1)}, u32[]{:S(2)}) copy-start(s32[8]{0:T(128)S(1)} %get-tuple-element.10) | copy-start | bytes 100
  32.4 151.6 %copy-start.11 = (s32[8]{0:T(128)}, s32[8]{0:T(128)S(1)}, u32[]{:S(2)}) copy-start(s32[8]{0:T(128)S(1)} %dynamic-slice_reduce_fusion) | copy-start | bytes 100
  99.2 86.1 %copy-start.3 = (bf16[8,3,256]{2,0,1:T(8,128)(2,1)S(1)}, bf16[8,3,256]{2,0,1:T(8,128)(2,1)}, u32[]{:S(2)}) copy-start(bf16[8,3,256]{2,0,1:T(8,128)(2,1)} %param.33) | copy-start | bytes 36868
  99.2 86.7 %copy-start.2 = (bf16[8,3,512]{2,0,1:T(8,128)(2,1)S(1)}, bf16[8,3,512]{2,0,1:T(8,128)(2,1)}, u32[]{:S(2)}) copy-start(bf16[8,3,512]{2,0,1:T(8,128)(2,1)} %param.32) | copy-start | bytes 73732
  184.7 17.2 %collective-permute-start = (bf16[2,16,776]{2,1,0:T(8,128)(2,1)S(1)}, bf16[2,16,776]{2,1,0:T(8,128)(2,1)S(1)}, u32[]{:S(2)}, u32[]{:S(2)}) collective-permute-start(bf16[2,16,776]{2,1,0:T(8,128)(2,1)S(1)} %slice.143), channel_id=1, source_target_pairs={{0,0},{8,8},{16,16},{24,24},{32,32},{40,40},{48,48},{56,56},{64,64... | collective-permute-start | bytes 149000 | tf_op jit(solution)/shard_map/ppermute | solution.py:16
  185.9 31.2 %copy-start.8 = (bf16[8,3,256]{2,1,0:T(4,128)(2,1)}, bf16[8,3,256]{2,1,0:T(4,128)(2,1)S(1)}, u32[]{:S(2)}) copy-start(bf16[8,3,256]{2,1,0:T(4,128)(2,1)S(1)} %copy.145) | copy-start | bytes 36868
  186.6 29.0 %copy-start.14 = (f32[8]{0:T(128)S(1)}, f32[8]{0:T(128)}, u32[]{:S(2)}) copy-start(f32[8]{0:T(128)} %param.24) | copy-start | bytes 100
  186.6 30.5 %copy-start.6 = (bf16[8,3,512]{2,1,0:T(4,128)(2,1)}, bf16[8,3,512]{2,1,0:T(4,128)(2,1)S(1)}, u32[]{:S(2)}) copy-start(bf16[8,3,512]{2,1,0:T(4,128)(2,1)S(1)} %copy.144) | copy-start | bytes 73732
  186.8 17.4 %collective-permute-start.1 = (bf16[2,16,776]{2,1,0:T(8,128)(2,1)S(1)}, bf16[2,16,776]{2,1,0:T(8,128)(2,1)S(1)}, u32[]{:S(2)}, u32[]{:S(2)}) collective-permute-start(bf16[2,16,776]{2,1,0:T(8,128)(2,1)S(1)} %slice.145), channel_id=1, source_target_pairs={{0,8},{8,16},{16,24},{24,32},{32,40},{40,48},{48,56},{56,64},{64,7... | collective-permute-start | bytes 149000 | tf_op jit(solution)/shard_map/ppermute | solution.py:16
  189.1 18.4 %collective-permute-start.2 = (bf16[2,16,776]{2,1,0:T(8,128)(2,1)S(1)}, bf16[2,16,776]{2,1,0:T(8,128)(2,1)S(1)}, u32[]{:S(2)}, u32[]{:S(2)}) collective-permute-start(bf16[2,16,776]{2,1,0:T(8,128)(2,1)S(1)} %slice.147), channel_id=1, source_target_pairs={{0,16},{8,24},{16,32},{24,40},{32,48},{40,56},{48,64},{56,72},{64,... | collective-permute-start | bytes 149000 | tf_op jit(solution)/shard_map/ppermute | solution.py:16
  192.7 18.0 %collective-permute-start.3 = (bf16[2,16,776]{2,1,0:T(8,128)(2,1)S(1)}, bf16[2,16,776]{2,1,0:T(8,128)(2,1)S(1)}, u32[]{:S(2)}, u32[]{:S(2)}) collective-permute-start(bf16[2,16,776]{2,1,0:T(8,128)(2,1)S(1)} %slice.149), channel_id=1, source_target_pairs={{0,24},{8,32},{16,40},{24,48},{32,56},{40,64},{48,72},{56,80},{64,... | collective-permute-start | bytes 149000 | tf_op jit(solution)/shard_map/ppermute | solution.py:16
  196.2 14.7 %collective-permute-start.4 = (bf16[2,16,776]{2,1,0:T(8,128)(2,1)S(1)}, bf16[2,16,776]{2,1,0:T(8,128)(2,1)S(1)}, u32[]{:S(2)}, u32[]{:S(2)}) collective-permute-start(bf16[2,16,776]{2,1,0:T(8,128)(2,1)S(1)} %slice.151), channel_id=1, source_target_pairs={{0,32},{8,40},{16,48},{24,56},{32,64},{40,72},{48,80},{56,88},{64,... | collective-permute-start | bytes 149000 | tf_op jit(solution)/shard_map/ppermute | solution.py:16
  201.9 8.9 %collective-permute-start.5 = (bf16[2,16,776]{2,1,0:T(8,128)(2,1)S(1)}, bf16[2,16,776]{2,1,0:T(8,128)(2,1)S(1)}, u32[]{:S(2)}, u32[]{:S(2)}) collective-permute-start(bf16[2,16,776]{2,1,0:T(8,128)(2,1)S(1)} %slice.153), channel_id=1, source_target_pairs={{0,40},{8,48},{16,56},{24,64},{32,72},{40,80},{48,88},{56,96},{64,... | collective-permute-start | bytes 149000 | tf_op jit(solution)/shard_map/ppermute | solution.py:16
  204.2 7.3 %collective-permute-start.6 = (bf16[2,16,776]{2,1,0:T(8,128)(2,1)S(1)}, bf16[2,16,776]{2,1,0:T(8,128)(2,1)S(1)}, u32[]{:S(2)}, u32[]{:S(2)}) collective-permute-start(bf16[2,16,776]{2,1,0:T(8,128)(2,1)S(1)} %slice.155), channel_id=1, source_target_pairs={{0,48},{8,56},{16,64},{24,72},{32,80},{40,88},{48,96},{56,104},{64... | collective-permute-start | bytes 149000 | tf_op jit(solution)/shard_map/ppermute | solution.py:16
  207.5 6.8 %collective-permute-start.7 = (bf16[2,16,776]{2,1,0:T(8,128)(2,1)S(1)}, bf16[2,16,776]{2,1,0:T(8,128)(2,1)S(1)}, u32[]{:S(2)}, u32[]{:S(2)}) collective-permute-start(bf16[2,16,776]{2,1,0:T(8,128)(2,1)S(1)} %slice.157), channel_id=1, source_target_pairs={{0,56},{8,64},{16,72},{24,80},{32,88},{40,96},{48,104},{56,112},{6... | collective-permute-start | bytes 149000 | tf_op jit(solution)/shard_map/ppermute | solution.py:16
  215.4 1.8 copy-start.4
  217.1 3.7 copy-start.1
  220.8 5.8 %copy-start.5 = (f32[8,16,8]{1,2,0:T(8,128)S(1)}, f32[8,16,8]{1,2,0:T(8,128)}, u32[]{:S(2)}) copy-start(f32[8,16,8]{1,2,0:T(8,128)} %copy.150) | copy-start | bytes 12292
  220.8 5.8 %copy-start.20 = (pred[8,16]{1,0:T(8,128)(4,1)S(1)}, pred[8,16]{1,0:T(8,128)(4,1)}, u32[]{:S(2)}) copy-start(pred[8,16]{1,0:T(8,128)(4,1)} %iota_compare_fusion.9) | copy-start | bytes 388
  220.9 5.9 %copy-start.15 = (f32[8]{0:T(128)S(1)}, f32[8]{0:T(128)}, u32[]{:S(2)}) copy-start(f32[8]{0:T(128)} %param.24) | copy-start | bytes 100
  220.9 5.9 %copy-start.19 = (pred[8,16]{1,0:T(8,128)(4,1)S(1)}, pred[8,16]{1,0:T(8,128)(4,1)}, u32[]{:S(2)}) copy-start(pred[8,16]{1,0:T(8,128)(4,1)} %iota_compare_fusion.8) | copy-start | bytes 388
  220.9 6.6 %copy-start.7 = (f32[8,16,16]{2,1,0:T(8,128)S(1)}, f32[8,16,16]{2,1,0:T(8,128)}, u32[]{:S(2)}) copy-start(f32[8,16,16]{2,1,0:T(8,128)} %fusion.29) | copy-start | bytes 24580
  220.9 6.6 %copy-start.18 = (pred[16,16]{1,0:T(8,128)(4,1)S(1)}, pred[16,16]{1,0:T(8,128)(4,1)}, u32[]{:S(2)}) copy-start(pred[16,16]{1,0:T(8,128)(4,1)} %iota_compare_fusion.3) | copy-start | bytes 772
  220.9 6.6 %copy-start.21 = (f32[8]{0:T(128)S(1)}, f32[8]{0:T(128)}, u32[]{:S(2)}) copy-start(f32[8]{0:T(128)} %param.26) | copy-start | bytes 100
  226.8 0.7 copy-start.10
  228.4 30.2 %copy-start.12 = (s32[8]{0:T(128)S(1)}, s32[8]{0:T(128)}, u32[]{:S(2)}) copy-start(s32[8]{0:T(128)} %copy-done.11) | copy-start | bytes 100
  232.5 13.4 %collective-permute-start.8 = (bf16[2,16,512]{2,1,0:T(8,128)(2,1)S(1)}, bf16[2,16,512]{2,1,0:T(8,128)(2,1)S(1)}, u32[]{:S(2)}, u32[]{:S(2)}) collective-permute-start(bf16[2,16,512]{2,1,0:T(8,128)(2,1)S(1)} %bitcast.104), channel_id=1, source_target_pairs={{0,0},{8,8},{16,16},{24,24},{32,32},{40,40},{48,48},{56,56},{64,64... | collective-permute-start | bytes 98312 | tf_op jit(solution)/shard_map/ppermute | solution.py:16
  232.6 17.7 %collective-permute-start.9 = (bf16[2,16,512]{2,1,0:T(8,128)(2,1)S(1)}, bf16[2,16,512]{2,1,0:T(8,128)(2,1)S(1)}, u32[]{:S(2)}, u32[]{:S(2)}) collective-permute-start(bf16[2,16,512]{2,1,0:T(8,128)(2,1)S(1)} %bitcast.103), channel_id=1, source_target_pairs={{0,504},{8,0},{16,8},{24,16},{32,24},{40,32},{48,40},{56,48},{64,5... | collective-permute-start | bytes 98312 | tf_op jit(solution)/shard_map/ppermute | solution.py:16
  236.2 16.0 %collective-permute-start.10 = (bf16[2,16,512]{2,1,0:T(8,128)(2,1)S(1)}, bf16[2,16,512]{2,1,0:T(8,128)(2,1)S(1)}, u32[]{:S(2)}, u32[]{:S(2)}) collective-permute-start(bf16[2,16,512]{2,1,0:T(8,128)(2,1)S(1)} %bitcast.102), channel_id=1, source_target_pairs={{0,496},{8,504},{16,0},{24,8},{32,16},{40,24},{48,32},{56,40},{64,... | collective-permute-start | bytes 98312 | tf_op jit(solution)/shard_map/ppermute | solution.py:16
  239.8 16.6 %collective-permute-start.11 = (bf16[2,16,512]{2,1,0:T(8,128)(2,1)S(1)}, bf16[2,16,512]{2,1,0:T(8,128)(2,1)S(1)}, u32[]{:S(2)}, u32[]{:S(2)}) collective-permute-start(bf16[2,16,512]{2,1,0:T(8,128)(2,1)S(1)} %bitcast.101), channel_id=1, source_target_pairs={{0,488},{8,496},{16,504},{24,0},{32,8},{40,16},{48,24},{56,32},{64... | collective-permute-start | bytes 98312 | tf_op jit(solution)/shard_map/ppermute | solution.py:16
  241.8 14.7 %collective-permute-start.12 = (bf16[2,16,512]{2,1,0:T(8,128)(2,1)S(1)}, bf16[2,16,512]{2,1,0:T(8,128)(2,1)S(1)}, u32[]{:S(2)}, u32[]{:S(2)}) collective-permute-start(bf16[2,16,512]{2,1,0:T(8,128)(2,1)S(1)} %bitcast.100), channel_id=1, source_target_pairs={{0,480},{8,488},{16,496},{24,504},{32,0},{40,8},{48,16},{56,24},{6... | collective-permute-start | bytes 98312 | tf_op jit(solution)/shard_map/ppermute | solution.py:16
  245.9 10.6 %collective-permute-start.13 = (bf16[2,16,512]{2,1,0:T(8,128)(2,1)S(1)}, bf16[2,16,512]{2,1,0:T(8,128)(2,1)S(1)}, u32[]{:S(2)}, u32[]{:S(2)}) collective-permute-start(bf16[2,16,512]{2,1,0:T(8,128)(2,1)S(1)} %bitcast.99), channel_id=1, source_target_pairs={{0,472},{8,480},{16,488},{24,496},{32,504},{40,0},{48,8},{56,16},{... | collective-permute-start | bytes 98312 | tf_op jit(solution)/shard_map/ppermute | solution.py:16
  250.3 6.7 %collective-permute-start.14 = (bf16[2,16,512]{2,1,0:T(8,128)(2,1)S(1)}, bf16[2,16,512]{2,1,0:T(8,128)(2,1)S(1)}, u32[]{:S(2)}, u32[]{:S(2)}) collective-permute-start(bf16[2,16,512]{2,1,0:T(8,128)(2,1)S(1)} %bitcast.98), channel_id=1, source_target_pairs={{0,464},{8,472},{16,480},{24,488},{32,496},{40,504},{48,0},{56,8},... | collective-permute-start | bytes 98312 | tf_op jit(solution)/shard_map/ppermute | solution.py:16
  252.2 6.2 %collective-permute-start.15 = (bf16[2,16,512]{2,1,0:T(8,128)(2,1)S(1)}, bf16[2,16,512]{2,1,0:T(8,128)(2,1)S(1)}, u32[]{:S(2)}, u32[]{:S(2)}) collective-permute-start(bf16[2,16,512]{2,1,0:T(8,128)(2,1)S(1)} %bitcast.97), channel_id=1, source_target_pairs={{0,456},{8,464},{16,472},{24,480},{32,488},{40,496},{48,504},{56,0... | collective-permute-start | bytes 98312 | tf_op jit(solution)/shard_map/ppermute | solution.py:16
  349.6 5.6 %copy-start.9 = (bf16[8,3,256]{2,1,0:T(4,128)(2,1)S(1)}, bf16[8,3,256]{2,1,0:T(4,128)(2,1)}, u32[]{:S(2)}) copy-start(bf16[8,3,256]{2,1,0:T(4,128)(2,1)} %copy-done.8) | copy-start | bytes 36868
Sparse Core Ops, SparseCore 0:
  11.4 86.2 all-gather.6
  101.0 80.6 all-gather.4
  185.0 80.6 all-gather.8
  268.9 80.6 all-gather.10
  353.3 39.0 reduce-scatter.1
